TPU v7x, 256 devices: a whole 4x4x8 slice. The times are simulated.
256 devices in a mesh: band: 4 (over z_hi, core), grid: 64 (over y, z_lo, x).
Axes of the slice: x: 4, y: 4, z: 8 (z_hi: 2, z_lo: 4; z = z_hi * 4 + z_lo), core: 2. Of those that a mesh axis runs over, the one named last changes fastest.
Arguments:
- orbitals: bfloat16 [256, 384, 32, 128], P('band', 'grid'), may hold values from -24 to 24, as said below
- potential: float32 [384, 32, 128], P('grid'), may hold values from -1 to 1
Outputs:
- gradient: float32 [256, 384, 32, 128], P('band', 'grid')
- intersection: float32 [256, 256], P('band')
- subspace: float32 [256, 256], P('band')
Inputs may be any that keep to these rules, and one draw needn't show every extreme that they name: `orbitals`: orbital values of order one.
All inputs are finite; a program needn't handle non-finite values.
Results may differ from a plain program's by a relative error of at most 0.0003.
Values may be sent and summed in bfloat16 or wider, within the bound.
A program may use at most 128 MiB of HBM per device.

v0:
```python
import jax
import jax.numpy as jnp
from jax import lax
from jax.sharding import PartitionSpec as P

COEFFS = (-49.0 / 18.0, 3.0 / 2.0, -3.0 / 20.0, 1.0 / 90.0)


def padded_2(cells, sides, width):
    for axis, dim in sides:
        count = lax.axis_size(axis)
        head = lax.slice_in_dim(cells, 0, width, axis=dim)
        tail = lax.slice_in_dim(cells, cells.shape[dim] - width, cells.shape[dim], axis=dim)
        cells = jnp.concatenate(
            [
                lax.ppermute(tail, axis, [(i, (i + 1) % count) for i in range(count)]),
                cells,
                lax.ppermute(head, axis, [((i + 1) % count, i) for i in range(count)]),
            ],
            axis=dim,
        )
    return cells


def apply_hamiltonian(padded, potential):
    stencil_reach = len(COEFFS) - 1
    width_x = padded.shape[1] - 2 * stencil_reach
    planes = padded.shape[2]
    center = padded[:, stencil_reach : stencil_reach + width_x].astype(jnp.float32)
    z_padded = jnp.pad(center, ((0, 0), (0, 0), (stencil_reach, stencil_reach), (0, 0)))
    total = 3.0 * COEFFS[0] * center
    for shift_by in range(1, stencil_reach + 1):
        pair_x = padded[:, stencil_reach + shift_by : stencil_reach + shift_by + width_x].astype(
            jnp.float32
        ) + padded[:, stencil_reach - shift_by : stencil_reach - shift_by + width_x].astype(
            jnp.float32
        )
        pair_z = (
            z_padded[:, :, stencil_reach + shift_by : stencil_reach + shift_by + planes]
            + z_padded[:, :, stencil_reach - shift_by : stencil_reach - shift_by + planes]
        )
        pair_y = jnp.roll(center, shift_by, 3) + jnp.roll(center, -shift_by, 3)
        total = total + COEFFS[shift_by] * (pair_x + pair_z + pair_y)
    return -0.5 * total + potential * center


def row_products(left, right):
    return lax.dot_general(
        left, right, (((1,), (1,)), ((), ())), preferred_element_type=jnp.float32
    )


def body(orbitals, potential):
    shape = orbitals.shape
    orb_dev = shape[0]
    cell_count = shape[1] * lax.axis_size("grid") * shape[2] * shape[3]
    group_count = orb_dev // 16
    stencil_reach = len(COEFFS) - 1
    padded = padded_2(orbitals, (("grid", 1),), stencil_reach)
    groups = padded.reshape((group_count, 16) + padded.shape[1:])
    hpsi = lax.map(lambda group: apply_hamiltonian(group, potential), groups).reshape(shape)
    flat_psi = orbitals.reshape(orb_dev, -1)
    flat_h = hpsi.astype(jnp.bfloat16).reshape(orb_dev, -1)
    panel_rows = lax.all_gather(flat_psi, "band", axis=0, tiled=True)
    s_rows = row_products(flat_psi, panel_rows)
    h_rows = row_products(flat_h, panel_rows)
    s_rows, h_rows = (s_rows, h_rows)
    s_summed, h_summed = lax.psum((s_rows, h_rows), "grid")
    intersection = s_summed / cell_count
    subspace = h_summed / cell_count
    offset_rows = lax.axis_index("band") * orb_dev
    s_diag = jnp.diagonal(lax.dynamic_slice_in_dim(intersection, offset_rows, orb_dev, 1))
    h_diag = jnp.diagonal(lax.dynamic_slice_in_dim(subspace, offset_rows, orb_dev, 1))
    rayleigh = h_diag / (s_diag + 1e-06)
    gradient = (hpsi - rayleigh[:, None, None, None] * orbitals.astype(jnp.float32)) / (
        2.0 + potential
    )
    return (gradient, intersection, subspace)


def solution(mesh):
    in_specs = (P("band", "grid", None, None), P("grid", None, None))
    out_specs = (P("band", "grid", None, None), P("band", None), P("band", None))
    return jax.shard_map(body, mesh=mesh, in_specs=in_specs, out_specs=out_specs, check_vma=False)
```

profile of v0, /device:TPU:2, one launch (start us, length us, event | category | flops | bytes accessed | tf_op | source)
XLA Modules:
  0.0 889.9 jit_solution(4659854884611012534)
XLA Ops:
  7.2 0.0 all-gather.2.cloned.1.call-start
  7.2 5.6 copy.8
  12.8 0.0 all-gather.2.cloned.1.call-update
  12.9 0.0 all-reduce.4.cloned.1.call-start
  12.9 1.8 copy-done
  14.7 2.3 fusion.27
  17.0 1.5 collective-permute-start
  18.5 0.8 collective-permute-start.1
  19.2 34.2 %collective-permute-done = bf16[64,3,32,128]{3,2,1,0:T(8,128)(2,1)} collective-permute-done((bf16[64,3,32,128]{3,2,1,0:T(8,128)(2,1)}, bf16[64,3,32,128]{3,2,1,0:T(8,128)(2,1)}, u32[]{:S(2)}, u32[]{:S(2)}) %collective-permute-start) | collective-permute-done | bytes 1572896 | tf_op jit(solution)/shard_map/ppermute | solution.py:16
  53.4 1.2 collective-permute-done.1
  54.6 5.0 pad_maximum_fusion
  59.6 59.5 %while.12 = (s32[]{:T(128)}, f32[4,16,6,32,128]{4,3,2,1,0:T(8,128)}, bf16[4,16,12,32,128]{4,3,2,1,0:T(8,128)(2,1)}, f32[6,32,128]{2,1,0:T(8,128)S(1)}, s32[]{:T(128)}) while((s32[]{:T(128)}, f32[4,16,6,32,128]{4,3,2,1,0:T(8,128)}, bf16[4,16,12,32,128]{4,3,2,1,0:T(8,128)(2,1)}, f32[6,32,128]{2,1,0:T(8,128)S(1)}, s32[]{:T(128)}) %tuple.59), condition=%wide.region_1.2_spmd, body=%wide.region_0.1_spmd.sunk | while | flops 14942210 | bytes 44888640 | solution.py:61
  59.6 1.7 dynamic-slice_bitcast_fusion.2
  61.3 0.2 slice_convert_fusion.2
  61.5 0.6 fusion.39
  62.1 0.6 fusion.40
  62.7 0.6 fusion.41
  63.3 0.6 fusion.42
  63.9 1.7 fusion.43
  65.6 2.3 fusion.44
  67.9 6.6 fusion.45
  74.5 1.7 dynamic-slice_bitcast_fusion.2
  76.2 0.2 slice_convert_fusion.2
  76.4 0.6 fusion.39
  77.0 0.6 fusion.40
  77.6 0.6 fusion.41
  78.2 0.6 fusion.42
  78.8 1.7 fusion.43
  80.5 2.3 fusion.44
  82.8 6.6 fusion.45
  89.4 1.7 dynamic-slice_bitcast_fusion.2
  91.1 0.2 slice_convert_fusion.2
  91.3 0.6 fusion.39
  91.9 0.6 fusion.40
  92.5 0.6 fusion.41
  93.1 0.6 fusion.42
  93.7 1.7 fusion.43
  95.4 2.2 fusion.44
  97.6 6.8 fusion.45
  104.4 1.7 dynamic-slice_bitcast_fusion.2
  106.1 0.2 slice_convert_fusion.2
  106.3 0.6 fusion.39
  106.9 0.6 fusion.40
  107.5 0.6 fusion.41
  108.0 0.6 fusion.42
  108.6 1.7 fusion.43
  110.4 2.2 fusion.44
  112.6 6.6 fusion.45
  119.2 5.3 convert_element_type.56
  124.5 5.0 convert_element_type.57
  129.5 46.6 %all-gather.2.cloned.1.call-done = bf16[256,24576]{1,0:T(8,128)(2,1)} async-done(((bf16[64,24576]{1,0:T(8,128)(2,1)}), bf16[256,24576]{1,0:T(8,128)(2,1)}) %all-gather.2.cloned.1.call-update) | async-done | bytes 12582928 | tf_op jit(solution)/shard_map/all_gather | solution.py:64
  176.2 0.0 copy-done.1
  176.2 9.3 %fusion.20 = f32[64,256]{1,0:T(8,128)} fusion(bf16[256,24576]{1,0:T(8,128)(2,1)} %all-gather.2.cloned.1.call-done, bf16[8,8,192,128]{3,2,1,0:T(8,128)(2,1)S(1)} %bitcast.29), kind=kOutput, calls=%fused_computation.43 | convolution fusion | flops 805306368 | bytes 15794176 | tf_op jit(solution)/shard_map/dot_general | solution.py:48
  185.5 9.1 %fusion.28 = f32[64,256]{1,0:T(8,128)} fusion(bf16[64,24576]{1,0:T(8,128)(2,1)S(1)} %copy-done.2, bf16[256,24576]{1,0:T(8,128)(2,1)} %all-gather.2.cloned.1.call-done), kind=kOutput, calls=%fused_computation.51 | convolution fusion | flops 805306368 | bytes 15794176 | tf_op jit(solution)/shard_map/dot_general | solution.py:48
  194.6 0.0 all-reduce.4.cloned.1.call-update
  194.6 678.5 %all-reduce.4.cloned.1.call-done = (f32[64,256]{1,0:T(8,128)}, f32[64,256]{1,0:T(8,128)}) async-done(((f32[64,256]{1,0:T(8,128)}, f32[64,256]{1,0:T(8,128)}), (f32[64,256]{1,0:T(8,128)}, f32[64,256]{1,0:T(8,128)})) %all-reduce.4.cloned.1.call-update) | async-done | bytes 131088 | tf_op jit(solution)/shard_map/psum | solution.py:68
  873.1 0.9 broadcast_multiply_fusion
  874.0 0.0 copy-start.4
  874.0 0.0 copy-start.5
  874.0 0.1 constant_dynamic-slice_fusion
  874.1 0.1 constant_dynamic-slice_fusion.1
  874.2 0.8 gather_fusion.1
  875.0 0.8 gather_fusion
  875.8 7.2 fusion.19
  (12 shorter events, 0.0 us)
Async XLA Ops:
  7.2 169.0 %all-gather.2.cloned.1.call-start = ((), (), s32[]{:S(2)}) async-start(), calls=%async_computation | async-start | bytes 15728640 | tf_op jit(solution)/shard_map/all_gather | solution.py:64
  12.8 1.9 copy-start
  12.9 860.3 %all-reduce.4.cloned.1.call-start = ((), (), s32[]{:S(2)}) async-start(), calls=%async_computation.1 | async-start | bytes 262144 | tf_op jit(solution)/shard_map/psum | solution.py:68
  17.0 36.5 %collective-permute-start = (bf16[64,3,32,128]{3,2,1,0:T(8,128)(2,1)}, bf16[64,3,32,128]{3,2,1,0:T(8,128)(2,1)}, u32[]{:S(2)}, u32[]{:S(2)}) collective-permute-start(bf16[64,3,32,128]{3,2,1,0:T(8,128)(2,1)} %get-tuple-element.79), channel_id=1, source_target_pairs={{0,1},{1,2},{2,3},{3,4},{4,5},{5,6},{6,7},{7,8},{8,9},{9,10},{10,1... | collective-permute-start | bytes 4718600 | tf_op jit(solution)/shard_map/ppermute | solution.py:16
  18.5 36.2 %collective-permute-start.1 = (bf16[64,3,32,128]{3,2,1,0:T(8,128)(2,1)}, bf16[64,3,32,128]{3,2,1,0:T(8,128)(2,1)}, u32[]{:S(2)}, u32[]{:S(2)}) collective-permute-start(bf16[64,3,32,128]{3,2,1,0:T(8,128)(2,1)} %get-tuple-element.80), channel_id=1, source_target_pairs={{1,0},{2,1},{3,2},{4,3},{5,4},{6,5},{7,6},{8,7},{9,8},{10,9},{11,1... | collective-permute-start | bytes 4718600 | tf_op jit(solution)/shard_map/ppermute | solution.py:18
  19.2 40.4 %copy-start.3 = (f32[6,32,128]{2,1,0:T(8,128)S(1)}, f32[6,32,128]{2,1,0:T(8,128)}, u32[]{:S(2)}) copy-start(f32[6,32,128]{2,1,0:T(8,128)} %param.5) | copy-start | bytes 294916
  124.5 51.6 %copy-start.1 = (bf16[64,6,32,128]{3,2,1,0:T(8,128)(2,1)S(1)}, bf16[64,6,32,128]{3,2,1,0:T(8,128)(2,1)}, u32[]{:S(2)}) copy-start(bf16[64,6,32,128]{3,2,1,0:T(8,128)(2,1)} %param.4) | copy-start | bytes 9437188
  176.2 9.3 %copy-start.2 = (bf16[64,24576]{1,0:T(8,128)(2,1)S(1)}, bf16[64,24576]{1,0:T(8,128)(2,1)}, u32[]{:S(2)}) copy-start(bf16[64,24576]{1,0:T(8,128)(2,1)} %convert_element_type.57) | copy-start | bytes 9437188
  874.0 9.0 %copy-start.4 = (f32[64,256]{1,0:T(8,128)}, f32[64,256]{1,0:T(8,128)S(1)}, u32[]{:S(2)}) copy-start(f32[64,256]{1,0:T(8,128)S(1)} %get-tuple-element.81) | copy-start | bytes 196612
  874.0 9.0 %copy-start.5 = (f32[64,256]{1,0:T(8,128)}, f32[64,256]{1,0:T(8,128)S(1)}, u32[]{:S(2)}) copy-start(f32[64,256]{1,0:T(8,128)S(1)} %get-tuple-element.82) | copy-start | bytes 196612
Sparse Core Ops, SparseCore 0:
  13.0 163.1 all-gather.1
  194.7 678.3 all-reduce.3
where the time goes:
time: 890 us
  waiting for transfers between devices  761 us (86%)
  local copies, waits for them, and re-layouts  48.4 us (5%)
  other arithmetic  45.8 us (5%)
  matrix products  18.4 us (2%)
  between operations  14.1 us (2%)
    psum x1, waiting for transfers between devices, body(): s_summed, h_summed = lax.psum((s_rows, h_rows), 'grid')  678 us
    all_gather x1, waiting for transfers between devices, body(): panel_rows = lax.all_gather(flat_psi, 'band', axis=0, tiled=True)  46.6 us
    ppermute x1, waiting for transfers between devices, padded_2(): lax.ppermute(tail, axis, [(i, (i + 1) % count) for i in range(count)])  34.2 us
    dynamic_update_slice x4, other arithmetic, body(): lax.map(lambda group: apply_hamiltonian(group, potential), groups)  26.6 us
    slice x24, local copies, waits for them, and re-layouts, apply_hamiltonian(): pair_y = jnp.roll(center, shift_by, 3) + jnp.roll(center, -shift_by, 3)  25.2 us
    dot_general x2, matrix products, row_products(): lax.dot_general(left, right, (((1,), (1,)), ((), ())), preferred_element_...  18.4 us
  transfers between devices with their start and end apart: 4, of which 4 were waited for; matrix products, arithmetic and copies ran while one was open for 9% of the time, Pallas kernels for 0%

commit v1 on v0

--- a/solution.py
+++ b/solution.py
@@ -2,6 +2,7 @@
 import jax.numpy as jnp
 from jax import lax
 from jax.sharding import PartitionSpec as P
+from jax.lax import all_to_all, axis_size
 
 COEFFS = (-49.0 / 18.0, 3.0 / 2.0, -3.0 / 20.0, 1.0 / 90.0)
 
@@ -61,7 +62,10 @@
     hpsi = lax.map(lambda group: apply_hamiltonian(group, potential), groups).reshape(shape)
     flat_psi = orbitals.reshape(orb_dev, -1)
     flat_h = hpsi.astype(jnp.bfloat16).reshape(orb_dev, -1)
-    panel_rows = lax.all_gather(flat_psi, "band", axis=0, tiled=True)
+    local_data_switch = lambda m, row_axis, row_dim: jnp.concatenate(
+        all_to_all(jnp.stack([m] * axis_size(row_axis), axis=0), row_axis, 0, 0), axis=row_dim
+    )
+    panel_rows = local_data_switch(flat_psi, "band", 0)
     s_rows = row_products(flat_psi, panel_rows)
     h_rows = row_products(flat_h, panel_rows)
     s_rows, h_rows = (s_rows, h_rows)

time: 890 us -> 1080 us (1.21)
  waiting for transfers between devices: 761 us -> 941 us
    all_to_all x0 -> x1, waiting for transfers between devices: none -> 163 us  [body(): all_to_all(jnp.stack([m] * axis_size(row_axis), axis=0), row_axis, 0, 0)]
    psum x1, waiting for transfers between devices: 678 us -> 742 us  [body(): s_summed, h_summed = lax.psum((s_rows, h_rows), 'grid')]
    all_gather x1 -> x0, waiting for transfers between devices: 46.6 us -> none  [body(): panel_rows = lax.all_gather(flat_psi, 'band', axis=0, tiled=True)]
  transfers between devices with their start and end apart: 4 -> 4, of which waited for: 4 -> 4; matrix products, arithmetic and copies ran while one was open for 9% -> 7% of each run, Pallas kernels for 0% -> 0%
where the time goes in v1:
time: 1080 us
  waiting for transfers between devices  941 us (87%)
  local copies, waits for them, and re-layouts  51.1 us (5%)
  other arithmetic  45.8 us (4%)
  matrix products  18.4 us (2%)
  between operations  14.1 us (1%)
    psum x1, waiting for transfers between devices, body(): s_summed, h_summed = lax.psum((s_rows, h_rows), 'grid')  742 us
    all_to_all x1, waiting for transfers between devices, body(): all_to_all(jnp.stack([m] * axis_size(row_axis), axis=0), row_axis, 0, 0)  163 us
    ppermute x1, waiting for transfers between devices, padded_2(): lax.ppermute(tail, axis, [(i, (i + 1) % count) for i in range(count)])  35.1 us
    dynamic_update_slice x4, other arithmetic, body(): lax.map(lambda group: apply_hamiltonian(group, potential), groups)  26.6 us
    slice x24, local copies, waits for them, and re-layouts, apply_hamiltonian(): pair_y = jnp.roll(center, shift_by, 3) + jnp.roll(center, -shift_by, 3)  25 us
  transfers between devices with their start and end apart: 4, of which 4 were waited for; matrix products, arithmetic and copies ran while one was open for 7% of the time, Pallas kernels for 0%

profile of v1, /device:TPU:2, one launch (start us, length us, event | category | flops | bytes accessed | tf_op | source)
XLA Modules:
  0.0 1081.5 jit_solution(5646459006486532567)
XLA Ops:
  7.2 3.9 copy.8
  11.1 6.1 stack.3
  17.2 8.7 all-to-all-start
  26.0 0.0 all-reduce.4.cloned.1.call-start
  26.0 0.0 copy-done
  26.0 2.2 fusion.27
  28.2 1.5 collective-permute-start
  29.7 0.5 collective-permute-start.1
  30.2 35.1 %collective-permute-done = bf16[64,3,32,128]{3,2,1,0:T(8,128)(2,1)} collective-permute-done((bf16[64,3,32,128]{3,2,1,0:T(8,128)(2,1)}, bf16[64,3,32,128]{3,2,1,0:T(8,128)(2,1)}, u32[]{:S(2)}, u32[]{:S(2)}) %collective-permute-start) | collective-permute-done | bytes 1572896 | tf_op jit(solution)/shard_map/ppermute | solution.py:17
  65.3 1.2 collective-permute-done.1
  66.5 5.0 pad_maximum_fusion
  71.5 59.6 %while.12 = (s32[]{:T(128)}, f32[4,16,6,32,128]{4,3,2,1,0:T(8,128)}, bf16[4,16,12,32,128]{4,3,2,1,0:T(8,128)(2,1)}, f32[6,32,128]{2,1,0:T(8,128)S(1)}, s32[]{:T(128)}) while((s32[]{:T(128)}, f32[4,16,6,32,128]{4,3,2,1,0:T(8,128)}, bf16[4,16,12,32,128]{4,3,2,1,0:T(8,128)(2,1)}, f32[6,32,128]{2,1,0:T(8,128)S(1)}, s32[]{:T(128)}) %tuple.57), condition=%wide.region_1.2_spmd, body=%wide.region_0.1_spmd.sunk | while | flops 14942210 | bytes 44888640 | solution.py:62
  71.5 1.7 dynamic-slice_bitcast_fusion.2
  73.3 0.2 slice_convert_fusion.2
  73.5 0.6 fusion.39
  74.1 0.6 fusion.40
  74.7 0.6 fusion.41
  75.2 0.6 fusion.42
  75.8 1.8 fusion.43
  77.6 2.2 fusion.44
  79.8 6.6 fusion.45
  86.4 1.7 dynamic-slice_bitcast_fusion.2
  88.2 0.2 slice_convert_fusion.2
  88.4 0.6 fusion.39
  89.0 0.6 fusion.40
  89.5 0.6 fusion.41
  90.1 0.6 fusion.42
  90.7 1.8 fusion.43
  92.4 2.2 fusion.44
  94.7 6.6 fusion.45
  101.3 1.7 dynamic-slice_bitcast_fusion.2
  103.0 0.2 slice_convert_fusion.2
  103.2 0.6 fusion.39
  103.8 0.6 fusion.40
  104.4 0.6 fusion.41
  105.0 0.6 fusion.42
  105.6 1.8 fusion.43
  107.3 2.2 fusion.44
  109.5 6.7 fusion.45
  116.2 1.7 dynamic-slice_bitcast_fusion.2
  118.0 0.2 slice_convert_fusion.2
  118.2 0.6 fusion.39
  118.8 0.6 fusion.40
  119.3 0.6 fusion.41
  119.9 0.6 fusion.42
  120.5 1.8 fusion.43
  122.3 2.2 fusion.44
  124.5 6.6 fusion.45
  131.1 5.3 convert_element_type.56
  136.4 5.0 convert_element_type.57
  141.4 162.7 %all-to-all-done = bf16[4,64,24576]{2,1,0:T(8,128)(2,1)} async-done(((bf16[4,64,24576]{2,1,0:T(8,128)(2,1)}), bf16[4,64,24576]{2,1,0:T(8,128)(2,1)}, u32[]{:S(2)}, u32[]{:S(2)}) %all-to-all-start) | async-done | bytes 12582944 | tf_op jit(solution)/shard_map/all_to_all | solution.py:66
  304.1 9.3 fusion.20
  313.4 9.1 fusion.28
  322.5 0.0 all-reduce.4.cloned.1.call-update
  322.5 742.2 %all-reduce.4.cloned.1.call-done = (f32[64,256]{1,0:T(8,128)}, f32[64,256]{1,0:T(8,128)}) async-done(((f32[64,256]{1,0:T(8,128)}, f32[64,256]{1,0:T(8,128)}), (f32[64,256]{1,0:T(8,128)}, f32[64,256]{1,0:T(8,128)})) %all-reduce.4.cloned.1.call-update) | async-done | bytes 131088 | tf_op jit(solution)/shard_map/psum | solution.py:72
  1064.7 0.9 broadcast_multiply_fusion
  1065.6 0.0 copy-start.4
  1065.6 0.0 copy-start.5
  1065.6 0.1 constant_dynamic-slice_fusion
  1065.7 0.1 constant_dynamic-slice_fusion.1
  1065.8 0.8 gather_fusion.1
  1066.6 0.8 gather_fusion
  1067.4 7.2 fusion.19
  1074.6 0.0 copy-done.4
  (12 shorter events, 0.0 us)
Async XLA Ops:
  17.2 8.7 copy-start
  17.2 286.8 %all-to-all-start = ((bf16[4,64,24576]{2,1,0:T(8,128)(2,1)}), bf16[4,64,24576]{2,1,0:T(8,128)(2,1)}, u32[]{:S(2)}, u32[]{:S(2)}) async-start(bf16[4,64,24576]{2,1,0:T(8,128)(2,1)} %stack.3), calls=%async_computation | async-start | bytes 25165824 | tf_op jit(solution)/shard_map/all_to_all | solution.py:66
  26.0 1038.7 %all-reduce.4.cloned.1.call-start = ((), (), s32[]{:S(2)}) async-start(), calls=%async_computation.1 | async-start | bytes 262144 | tf_op jit(solution)/shard_map/psum | solution.py:72
  28.2 37.1 %collective-permute-start = (bf16[64,3,32,128]{3,2,1,0:T(8,128)(2,1)}, bf16[64,3,32,128]{3,2,1,0:T(8,128)(2,1)}, u32[]{:S(2)}, u32[]{:S(2)}) collective-permute-start(bf16[64,3,32,128]{3,2,1,0:T(8,128)(2,1)} %get-tuple-element.79), channel_id=1, source_target_pairs={{0,1},{1,2},{2,3},{3,4},{4,5},{5,6},{6,7},{7,8},{8,9},{9,10},{10,1... | collective-permute-start | bytes 4718600 | tf_op jit(solution)/shard_map/ppermute | solution.py:17
  29.7 36.8 %collective-permute-start.1 = (bf16[64,3,32,128]{3,2,1,0:T(8,128)(2,1)}, bf16[64,3,32,128]{3,2,1,0:T(8,128)(2,1)}, u32[]{:S(2)}, u32[]{:S(2)}) collective-permute-start(bf16[64,3,32,128]{3,2,1,0:T(8,128)(2,1)} %get-tuple-element.80), channel_id=1, source_target_pairs={{1,0},{2,1},{3,2},{4,3},{5,4},{6,5},{7,6},{8,7},{9,8},{10,9},{11,1... | collective-permute-start | bytes 4718600 | tf_op jit(solution)/shard_map/ppermute | solution.py:19
  30.2 41.3 %copy-start.3 = (f32[6,32,128]{2,1,0:T(8,128)S(1)}, f32[6,32,128]{2,1,0:T(8,128)}, u32[]{:S(2)}) copy-start(f32[6,32,128]{2,1,0:T(8,128)} %param.5) | copy-start | bytes 294916
  136.4 167.6 %copy-start.1 = (bf16[64,6,32,128]{3,2,1,0:T(8,128)(2,1)S(1)}, bf16[64,6,32,128]{3,2,1,0:T(8,128)(2,1)}, u32[]{:S(2)}) copy-start(bf16[64,6,32,128]{3,2,1,0:T(8,128)(2,1)} %param.4) | copy-start | bytes 9437188
  304.1 9.3 copy-start.2
  1065.6 9.0 copy-start.4
  1065.6 9.0 copy-start.5
Sparse Core Ops, SparseCore 0:
  322.6 742.0 all-reduce.3
